TPU v7x, 32 devices: a whole 2x2x4 slice. The times are simulated.
32 devices in a mesh: group: 4 (over y, x), tile: 4 (over z), video: 2 (over core).
Axes of the slice: x: 2, y: 2, z: 4, core: 2. Of those that a mesh axis runs over, the one named last changes fastest.
Arguments:
- features: bfloat16 [8, 8, 16, 24, 384], P(('video', 'tile'), 'group'), parts along dimension 0, may hold values from -6 to 6
- group_slot: int32 [4], replicated, may hold values from 0 to 3, each once
- margins: int32 [4, 4], P('tile'), may hold values from 0 to 4, as said below
- norm_gain: float32 [384], replicated, may hold values from 0.1 to 1.9
- kernel: bfloat16 [3, 3, 3, 384, 384], replicated, may hold values from -0.0625 to 0.0625
- conv_bias: float32 [384], replicated, may hold values from -3 to 3
Outputs:
- decoded: bfloat16 [8, 8, 16, 24, 384], P(('video', 'tile'), 'group'), parts along dimension 0
There are 2 independent parts, one for each index of `video`. A program takes and returns all parts, laid end to end along the dimension named above; an argument that names none is the same for every part. Nothing has to cross between parts.
Inputs may be any that keep to these rules, and one draw needn't show every extreme that they name: group_slot is a permutation of 0 to 3. margins[t] is (left, right, up, down) of tile t; a margin is 0 exactly at the image's border and 1 to 4 elsewhere; the margin a tile has toward a neighbour equals the neighbour's margin back; left and right margins depend only on the tile's column, up and down margins are the same for all columns; some margin equals 4.
All inputs are finite; a program needn't handle non-finite values.
Results may differ from a plain program's by a relative error of at most 0.0043.
Values may be sent and summed in bfloat16 or wider, within the bound.
A program may use at most 128 MiB of HBM per device.

v0:
```python
import jax
import jax.numpy as jnp
from jax import lax
from jax.sharding import PartitionSpec as P

M = 4
GRID_R = 2


def passed_along(shard, axis, by):
    peers = lax.axis_size(axis)
    pairs = [(i, i + by) for i in range(peers) if 0 <= i + by < peers]
    return lax.ppermute(shard, axis, pairs)


def activate(values, norm_gain):
    widened = values.astype(jnp.float32)
    inv_norm = lax.rsqrt(jnp.mean(widened * widened, axis=-1, keepdims=True) + 1e-06)
    return jax.nn.silu(widened * inv_norm * norm_gain).astype(jnp.bfloat16)


def convolve(padded, kernel, conv_bias, row_count, col_count):
    frame_count = padded.shape[0] - 2
    channels = padded.shape[-1]
    summed = jnp.zeros((frame_count * row_count * col_count, kernel.shape[-1]), jnp.float32)
    for tap_time in range(3):
        for tap_row in range(3):
            window = padded[tap_time : tap_time + frame_count, tap_row : tap_row + row_count]
            stacked = jnp.concatenate(
                [window[:, :, tap_col : tap_col + col_count] for tap_col in range(3)], axis=-1
            )
            flattened = stacked.reshape(frame_count * row_count * col_count, 3 * channels)
            summed = summed + jnp.dot(
                flattened,
                kernel[tap_time, tap_row].reshape(3 * channels, -1),
                preferred_element_type=jnp.float32,
            )
    return summed.reshape(frame_count, row_count, col_count, -1) + conv_bias


def window_band(core, near, far):
    position = jnp.arange(core + 2 * M, dtype=jnp.int32)
    return (position >= M - near) & (position < M + core + far)


def rim_weight(step, core, near, far):
    position = jnp.arange(core, dtype=jnp.int32)
    if step == 1:
        distance = position + 1
        margin = near
    elif step == -1:
        distance = core - position
        margin = far
    else:
        return jnp.ones((core,), jnp.float32)
    margin_f = margin.astype(jnp.float32)
    return jnp.maximum(margin_f + 1.0 - distance.astype(jnp.float32), 0.0) / (margin_f + 1.0)


def rim_source(step, core):
    if step == 1:
        return (core - M, M, 0)
    if step == -1:
        return (0, M, M + core)
    return (0, core, M)


def panel_source(step, core):
    if step == 1:
        return (M + core, M, 0)
    if step == -1:
        return (0, M, core - M)
    return (M, core, 0)


def blend_add(weighted, weight_sum, panel, step_r, step_c, row_dest, col_dest, reaches):
    core_h = weighted.shape[1]
    core_w = weighted.shape[2]
    row_len = panel.shape[1]
    col_len = panel.shape[2]
    placed = jnp.pad(
        panel.astype(jnp.float32),
        (
            (0, 0),
            (row_dest, core_h - row_dest - row_len),
            (col_dest, core_w - col_dest - col_len),
            (0, 0),
        ),
    )
    weight = (
        rim_weight(step_r, core_h, reaches[2], reaches[3])[:, None]
        * rim_weight(step_c, core_w, reaches[0], reaches[1])[None, :]
    )
    return (weighted + placed * weight[None, :, :, None], weight_sum + weight)


def gather_rims(source_block, grid_cols):
    core_h = source_block.shape[1]
    core_w = source_block.shape[2]
    result = jnp.pad(source_block, ((0, 0), (M, M), (M, M), (0, 0)))
    for step_r in (1, 0, -1):
        for step_c in (1, 0, -1):
            if step_r == 0 and step_c == 0:
                continue
            row_first, row_len, row_dest = rim_source(step_r, core_h)
            col_first, col_len, col_dest = rim_source(step_c, core_w)
            outgoing = source_block[
                :, row_first : row_first + row_len, col_first : col_first + col_len
            ]
            incoming = passed_along(outgoing, "tile", step_r * grid_cols + step_c)
            result = result.at[:, row_dest : row_dest + row_len, col_dest : col_dest + col_len].set(
                incoming
            )
    return result


def local(features, group_slot, margins, norm_gain, kernel, conv_bias):
    own_block = features[0]
    frame_count, core_h, core_w, channels = own_block.shape
    grid_cols = lax.axis_size("tile") // GRID_R
    reaches = margins[0]
    wanted = group_slot[lax.axis_index("group")] - 1
    chosen = jnp.zeros((2, core_h, core_w, channels), jnp.bfloat16)
    pieces = lax.all_gather(own_block[None], "group", axis=0, tiled=True)
    first_dev = jnp.int32(0)
    for offset in range(pieces.shape[0]):
        matches = group_slot[first_dev + offset] == wanted
        chosen = chosen + jnp.where(matches, pieces[offset], jnp.zeros_like(pieces[offset]))
    buffered = gather_rims(jnp.concatenate([chosen, own_block], axis=0), grid_cols)
    activated = activate(buffered, norm_gain)
    padded = jnp.pad(activated, ((0, 0), (1, 1), (1, 1), (0, 0)))
    weighted = jnp.zeros((frame_count, core_h, core_w, channels), jnp.float32)
    weight_sum = jnp.zeros((core_h, core_w), jnp.float32)
    inside = (
        window_band(core_h, reaches[2], reaches[3])[:, None]
        & window_band(core_w, reaches[0], reaches[1])[None, :]
    )
    inside = jnp.pad(inside, 1)
    masked = jnp.where(inside[None, :, :, None], padded, jnp.zeros_like(padded))
    outputs = convolve(masked, kernel, conv_bias, core_h + 2 * M, core_w + 2 * M).astype(
        jnp.bfloat16
    )
    for step_r in (1, 0, -1):
        for step_c in (1, 0, -1):
            row_first, row_len, row_dest = panel_source(step_r, core_h)
            col_first, col_len, col_dest = panel_source(step_c, core_w)
            outgoing = outputs[:, row_first : row_first + row_len, col_first : col_first + col_len]
            if step_r == 0 and step_c == 0:
                incoming = outgoing
            else:
                incoming = passed_along(outgoing, "tile", step_r * grid_cols + step_c)
            weighted, weight_sum = blend_add(
                weighted, weight_sum, incoming, step_r, step_c, row_dest, col_dest, reaches
            )
    return (weighted / weight_sum[None, :, :, None]).astype(jnp.bfloat16)[None]


def solution(mesh):
    return jax.shard_map(
        local,
        mesh=mesh,
        in_specs=(
            P(("video", "tile"), "group", None, None, None),
            P(),
            P("tile", None),
            P(),
            P(),
            P(),
        ),
        out_specs=P(("video", "tile"), "group", None, None, None),
        check_vma=False,
    )
```

profile of v0, /device:TPU:0, one launch (start us, length us, event | category | flops | bytes accessed | tf_op | source)
XLA Modules:
  0.0 182.1 jit_solution(15480783370561871145)
XLA Ops:
  7.3 1.4 fusion.30
  11.4 1.5 fusion.29
  20.3 1.4 and_reduce_fusion.1
  21.7 1.4 and_reduce_fusion
  23.2 5.7 %fusion.21 = (bf16[1,1,3,384,384]{4,3,2,1,0:T(8,128)(2,1)}, bf16[1,1,3,384,384]{4,3,2,1,0:T(8,128)(2,1)}, bf16[1,1,3,384,384]{4,3,2,1,0:T(8,128)(2,1)}, bf16[1,1...) fusion(bf16[3,3,3,384,384]{4,3,2,1,0:T(8,128)(2,1)} %param.26), kind=kLoop, calls=%fused_computation.92 | loop fusion | bytes 15925248 | tf_op jit(solution)/shard_map/slice | solution.py:35
  28.9 20.4 %all-gather.2.cloned.1.call-done = bf16[4,2,16,24,384]{4,3,2,1,0:T(8,128)(2,1)} async-done(((bf16[1,2,16,24,384]{4,3,2,1,0:T(8,128)(2,1)}), bf16[4,2,16,24,384]{4,3,2,1,0:T(8,128)(2,1)}) %all-gather.2.cloned.1.call-update) | async-done | bytes 2359312 | tf_op jit(solution)/shard_map/all_gather | solution.py:124
  49.3 1.8 fusion.9
  51.3 4.3 %collective-permute-start.1 = (bf16[4,4,24,384]{3,2,1,0:T(8,128)(2,1)S(1)}, bf16[4,4,24,384]{3,2,1,0:T(8,128)(2,1)S(1)}, u32[]{:S(2)}, u32[]{:S(2)}) collective-permute-start(bf16[4,4,24,384]{3,2,1,0:T(8,128)(2,1)S(1)} %get-tuple-element.150), channel_id=1, source_target_pairs={{0,4},{2,6},{1,5},{3,7},{8,12},{10,14},{9,13},{11,15},{16,20},{18,... | collective-permute-start | bytes 884744 | tf_op jit(solution)/shard_map/ppermute | solution.py:13
  56.4 2.2 %collective-permute-start = (bf16[4,4,4,384]{3,2,1,0:T(4,128)(2,1)S(1)}, bf16[4,4,4,384]{3,2,1,0:T(4,128)(2,1)S(1)}, u32[]{:S(2)}, u32[]{:S(2)}) collective-permute-start(bf16[4,4,4,384]{3,2,1,0:T(4,128)(2,1)S(1)} %get-tuple-element.146), channel_id=1, source_target_pairs={{0,6},{1,7},{8,14},{9,15},{16,22},{17,23},{24,30},{25,31}} | collective-permute-start | bytes 147464 | tf_op jit(solution)/shard_map/ppermute | solution.py:13
  58.8 1.3 collective-permute-start.7
  60.1 2.4 %collective-permute-start.2 = (bf16[4,4,4,384]{3,2,1,0:T(4,128)(2,1)}, bf16[4,4,4,384]{3,2,1,0:T(4,128)(2,1)}, u32[]{:S(2)}, u32[]{:S(2)}) collective-permute-start(bf16[4,4,4,384]{3,2,1,0:T(4,128)(2,1)} %get-tuple-element.147), channel_id=1, source_target_pairs={{0,2},{2,4},{4,6},{1,3},{3,5},{5,7},{8,10},{10,12},{12,14},{9,11},... | collective-permute-start | bytes 147464 | tf_op jit(solution)/shard_map/ppermute | solution.py:13
  62.5 1.3 collective-permute-start.5
  64.6 1.3 collective-permute-start.4
  66.0 7.2 %collective-permute-start.3 = (bf16[4,16,4,384]{3,2,1,0:T(4,128)(2,1)S(1)}, bf16[4,16,4,384]{3,2,1,0:T(4,128)(2,1)}, u32[]{:S(2)}, u32[]{:S(2)}) collective-permute-start(bf16[4,16,4,384]{3,2,1,0:T(4,128)(2,1)S(1)} %get-tuple-element.152), channel_id=1, source_target_pairs={{0,2},{2,4},{4,6},{1,3},{3,5},{5,7},{8,10},{10,12},{12,14},{9,11},... | collective-permute-start | bytes 589832 | tf_op jit(solution)/shard_map/ppermute | solution.py:13
  73.2 1.9 %dynamic-slice_select_fusion = bf16[4,4,24,384]{3,2,1,0:T(8,128)(2,1)S(1)} fusion(bf16[4,4,24,384]{3,2,1,0:T(8,128)(2,1)S(1)} %collective-permute-done.1, bf16[4,24,32,384]{3,2,1,0:T(8,128)(2,1)S(1)} %constant_dynamic-update-slice_fusion.4, s32[]{:T(128)} %bitcast.10, s32[]{:T(128)} %bitcast.11, pred[]{:T(512)} %and_reduce_fusion.1), kind=kLoop, calls=%fused_computation.58 | loop fusion | flops 147456 | bytes 884745 | tf_op jit(solution)/shard_map/select.9
  75.1 2.3 %scatter.29 = bf16[4,24,32,384]{3,2,1,0:T(8,128)(2,1)S(1)} dynamic-update-slice(bf16[4,24,32,384]{3,2,1,0:T(8,128)(2,1)S(1)} %constant_dynamic-update-slice_fusion.4, bf16[4,4,24,384]{3,2,1,0:T(8,128)(2,1)S(1)} %dynamic-slice_select_fusion, s32[]{:T(128)} %constant.276.clone.1, s32[]{:T(128)} %bitcast.10, s32[]{:T(128)} %bitcast.11, s32[]{:T(128)} %constant.276.clone.1) | dynamic-update-slice | bytes 589828 | tf_op jit(solution)/shard_map/scatter | solution.py:111
  77.5 1.5 collective-permute-start.6
  79.0 3.4 %dynamic-slice_select_fusion.1 = bf16[4,4,4,384]{3,2,1,0:T(4,128)(2,1)} fusion(bf16[4,4,4,384]{3,2,1,0:T(4,128)(2,1)} %collective-permute-done.2, bf16[4,24,32,384]{3,2,1,0:T(8,128)(2,1)S(1)} %scatter.29, s32[]{:T(128)} %bitcast.12, s32[]{:T(128)} %bitcast.13, pred[]{:T(512)} %and_reduce_fusion), kind=kLoop, calls=%fused_computation.66 | loop fusion | flops 24576 | bytes 147465 | tf_op jit(solution)/shard_map/select.10
  82.3 2.2 %scatter.30 = bf16[4,24,32,384]{3,2,1,0:T(8,128)(2,1)S(1)} dynamic-update-slice(bf16[4,24,32,384]{3,2,1,0:T(8,128)(2,1)S(1)} %scatter.29, bf16[4,4,4,384]{3,2,1,0:T(4,128)(2,1)} %dynamic-slice_select_fusion.1, s32[]{:T(128)} %constant.276.clone.1, s32[]{:T(128)} %bitcast.12, s32[]{:T(128)} %bitcast.13, s32[]{:T(128)} %constant.276.clone.1) | dynamic-update-slice | bytes 98308 | tf_op jit(solution)/shard_map/scatter | solution.py:111
  84.6 1.1 constant_dynamic-update-slice_fusion.3
  86.6 8.5 %collective-permute-done.6 = bf16[4,4,24,384]{3,2,1,0:T(8,128)(2,1)S(1)} collective-permute-done((bf16[4,4,24,384]{3,2,1,0:T(8,128)(2,1)S(1)}, bf16[4,4,24,384]{3,2,1,0:T(8,128)(2,1)S(1)}, u32[]{:S(2)}, u32[]{:S(2)}) %collective-permute-start.6) | collective-permute-done | bytes 294944 | tf_op jit(solution)/shard_map/ppermute | solution.py:13
  95.1 1.2 scatter.36
  97.7 2.2 %fusion.7 = bf16[4,24,32,384]{3,2,1,0:T(8,128)(2,1)S(1)} fusion(bf16[4,24,32,384]{3,2,1,0:T(8,128)(2,1)S(1)} %constant_dynamic-update-slice_fusion, f32[384]{0:T(512)} %param.25, f32[4,24,32]{2,1,0:T(8,128)S(1)} %add_rsqrt_fusion), kind=kLoop, calls=%fused_computation.9 | loop fusion | flops 9437184 | bytes 4732416 | tf_op jit(solution)/shard_map/convert_element_type | solution.py:19
  99.9 1.5 pad_select_fusion
  101.5 4.5 %fusion.23 = (bf16[2,24,32,384]{3,2,1,0:T(8,128)(2,1)S(1)}, bf16[2,24,32,384]{3,2,1,0:T(8,128)(2,1)S(1)}, bf16[2,24,32,384]{3,2,1,0:T(8,128)(2,1)}, bf16[2,24,32...) fusion(bf16[4,26,34,384]{3,2,1,0:T(8,128)(2,1)S(1)} %pad_select, ...), kind=kLoop, calls=%fused_computation.94 | loop fusion | bytes 18874368 | tf_op jit(solution)/shard_map/slice | solution.py:30
  105.9 6.3 %fusion.22 = (bf16[2,24,32,384]{3,2,1,0:T(8,128)(2,1)}, bf16[2,24,32,384]{3,2,1,0:T(8,128)(2,1)}, bf16[2,24,32,384]{3,2,1,0:T(8,128)(2,1)}, bf16[2,24,32,384]{3,...) fusion(bf16[4,26,34,384]{3,2,1,0:T(8,128)(2,1)S(1)} %pad_select, ...), kind=kLoop, calls=%fused_computation.93 | loop fusion | bytes 44826624 | tf_op jit(solution)/shard_map/slice | solution.py:30
  112.2 3.4 %pad_maximum_fusion = (bf16[2,24,32,1152]{3,2,1,0:T(8,128)(2,1)S(1)}, bf16[2,24,32,1152]{3,2,1,0:T(8,128)(2,1)S(1)}) fusion(bf16[2,24,32,384]{3,2,1,0:T(8,128)(2,1)} %get-tuple-element.134, bf16[2,24,32,384]{3,2,1,0:T(8,128)(2,1)} %get-tuple-element.135, bf16[2,24,32,384]{3,2,1,0:T(8,128)(2,1)} %get-tuple-element.136, ...), kind=kLoop, calls=%fused_computation.10 | loop fusion | flops 21233664 | bytes 14155776 | tf_op jit(solution)/shard_map/concatenate | solution.py:29
  115.7 2.1 %fusion.31 = f32[1536,384]{1,0:T(8,128)S(1)} fusion(bf16[1536,1152]{1,0:T(8,128)(2,1)S(1)} %bitcast.69, bf16[1152,384]{1,0:T(8,128)(2,1)S(1)} %bitcast.80), kind=kOutput, calls=%fused_computation.102 | convolution fusion | flops 1358954496 | bytes 6782976 | tf_op jit(solution)/shard_map/dot_general | solution.py:33
  117.8 3.6 %convolution_add_fusion.7 = f32[1536,384]{1,0:T(8,128)} fusion(f32[1536,384]{1,0:T(8,128)S(1)} %fusion.31, bf16[1536,1152]{1,0:T(8,128)(2,1)S(1)} %bitcast.65, bf16[1152,384]{1,0:T(8,128)(2,1)S(1)} %bitcast.79), kind=kOutput, calls=%fused_computation.27 | convolution fusion | flops 1359544320 | bytes 9142272 | tf_op jit(solution)/shard_map/dot_general | solution.py:33
  121.5 1.9 %pad_maximum_fusion.8 = bf16[2,24,32,1152]{3,2,1,0:T(8,128)(2,1)} fusion(bf16[2,24,32,384]{3,2,1,0:T(8,128)(2,1)S(1)} %copy-done.3, bf16[2,24,32,384]{3,2,1,0:T(8,128)(2,1)S(1)} %copy-done.4, bf16[2,24,32,384]{3,2,1,0:T(8,128)(2,1)S(1)} %copy-done.2), kind=kLoop, calls=%fused_computation.18 | loop fusion | flops 10616832 | bytes 7077888 | tf_op jit(solution)/shard_map/concatenate | solution.py:29
  124.6 3.9 %convolution_add_fusion.6 = f32[1536,384]{1,0:T(8,128)S(1)} fusion(f32[1536,384]{1,0:T(8,128)} %convolution_add_fusion.7, bf16[1536,1152]{1,0:T(8,128)(2,1)S(1)} %bitcast.66, bf16[1152,384]{1,0:T(8,128)(2,1)S(1)} %bitcast.78), kind=kOutput, calls=%fused_computation.26 | convolution fusion | flops 1359544320 | bytes 9142272 | tf_op jit(solution)/shard_map/dot_general | solution.py:33
  128.5 2.2 %convolution_add_fusion.5 = f32[1536,384]{1,0:T(8,128)S(1)} fusion(f32[1536,384]{1,0:T(8,128)S(1)} %convolution_add_fusion.6, bf16[1536,1152]{1,0:T(8,128)(2,1)S(1)} %bitcast.62, bf16[1152,384]{1,0:T(8,128)(2,1)S(1)} %bitcast.77), kind=kOutput, calls=%fused_computation.25 | convolution fusion | flops 1359544320 | bytes 9142272 | tf_op jit(solution)/shard_map/dot_general | solution.py:33
  131.9 2.2 %convolution_add_fusion.4 = f32[1536,384]{1,0:T(8,128)S(1)} fusion(f32[1536,384]{1,0:T(8,128)S(1)} %convolution_add_fusion.5, bf16[1536,1152]{1,0:T(8,128)(2,1)S(1)} %bitcast.67, bf16[1152,384]{1,0:T(8,128)(2,1)S(1)} %bitcast.76), kind=kOutput, calls=%fused_computation.24 | convolution fusion | flops 1359544320 | bytes 9142272 | tf_op jit(solution)/shard_map/dot_general | solution.py:33
  134.0 2.1 %convolution_add_fusion.3 = f32[1536,384]{1,0:T(8,128)S(1)} fusion(f32[1536,384]{1,0:T(8,128)S(1)} %convolution_add_fusion.4, bf16[1536,1152]{1,0:T(8,128)(2,1)S(1)} %bitcast.63, bf16[1152,384]{1,0:T(8,128)(2,1)S(1)} %bitcast.75), kind=kOutput, calls=%fused_computation.23 | convolution fusion | flops 1359544320 | bytes 9142272 | tf_op jit(solution)/shard_map/dot_general | solution.py:33
  137.4 2.2 %convolution_add_fusion.2 = f32[1536,384]{1,0:T(8,128)S(1)} fusion(f32[1536,384]{1,0:T(8,128)S(1)} %convolution_add_fusion.3, bf16[1536,1152]{1,0:T(8,128)(2,1)S(1)} %bitcast.68, bf16[1152,384]{1,0:T(8,128)(2,1)S(1)} %bitcast.74), kind=kOutput, calls=%fused_computation.22 | convolution fusion | flops 1359544320 | bytes 9142272 | tf_op jit(solution)/shard_map/dot_general | solution.py:33
  139.6 2.1 %convolution_add_fusion.1 = f32[1536,384]{1,0:T(8,128)S(1)} fusion(f32[1536,384]{1,0:T(8,128)S(1)} %convolution_add_fusion.2, bf16[1536,1152]{1,0:T(8,128)(2,1)S(1)} %bitcast.64, bf16[1152,384]{1,0:T(8,128)(2,1)S(1)} %bitcast.73), kind=kOutput, calls=%fused_computation.21 | convolution fusion | flops 1359544320 | bytes 9142272 | tf_op jit(solution)/shard_map/dot_general | solution.py:33
  141.8 2.1 %convolution_add_fusion = f32[1536,384]{1,0:T(8,128)S(1)} fusion(f32[1536,384]{1,0:T(8,128)S(1)} %convolution_add_fusion.1, bf16[1536,1152]{1,0:T(8,128)(2,1)S(1)} %bitcast.70, bf16[1152,384]{1,0:T(8,128)(2,1)S(1)} %bitcast.72), kind=kOutput, calls=%fused_computation.20 | convolution fusion | flops 1359544320 | bytes 9142272 | tf_op jit(solution)/shard_map/dot_general | solution.py:33
  144.4 1.3 collective-permute-start.8
  145.7 1.3 collective-permute-start.15
  147.0 1.3 collective-permute-start.13
  148.4 4.5 %collective-permute-start.10 = (bf16[2,4,4,384]{3,2,1,0:T(4,128)(2,1)S(1)}, bf16[2,4,4,384]{3,2,1,0:T(4,128)(2,1)S(1)}, u32[]{:S(2)}, u32[]{:S(2)}) collective-permute-start(bf16[2,4,4,384]{3,2,1,0:T(4,128)(2,1)S(1)} %get-tuple-element.140), channel_id=1, source_target_pairs={{0,2},{2,4},{4,6},{1,3},{3,5},{5,7},{8,10},{10,12},{12,14},{9,11},... | collective-permute-start | bytes 73736 | tf_op jit(solution)/shard_map/ppermute | solution.py:13
  152.9 1.9 %collective-permute-start.11 = (bf16[2,16,4,384]{3,2,1,0:T(4,128)(2,1)S(1)}, bf16[2,16,4,384]{3,2,1,0:T(4,128)(2,1)S(1)}, u32[]{:S(2)}, u32[]{:S(2)}) collective-permute-start(bf16[2,16,4,384]{3,2,1,0:T(4,128)(2,1)S(1)} %get-tuple-element.143), channel_id=1, source_target_pairs={{0,2},{2,4},{4,6},{1,3},{3,5},{5,7},{8,10},{10,12},{12,14},{9,11},... | collective-permute-start | bytes 294920 | tf_op jit(solution)/shard_map/ppermute | solution.py:13
  154.9 1.3 collective-permute-start.12
  156.2 6.9 %collective-permute-start.9 = (bf16[2,4,24,384]{3,2,1,0:T(8,128)(2,1)S(1)}, bf16[2,4,24,384]{3,2,1,0:T(8,128)(2,1)S(1)}, u32[]{:S(2)}, u32[]{:S(2)}) collective-permute-start(bf16[2,4,24,384]{3,2,1,0:T(8,128)(2,1)S(1)} %get-tuple-element.141), channel_id=1, source_target_pairs={{0,4},{2,6},{1,5},{3,7},{8,12},{10,14},{9,13},{11,15},{16,20},{18,... | collective-permute-start | bytes 442376 | tf_op jit(solution)/shard_map/ppermute | solution.py:13
  163.1 1.3 collective-permute-start.14
  164.5 1.2 collective-permute-done.9
  165.7 7.4 %collective-permute-done.14 = bf16[2,4,24,384]{3,2,1,0:T(8,128)(2,1)S(1)} collective-permute-done((bf16[2,4,24,384]{3,2,1,0:T(8,128)(2,1)S(1)}, bf16[2,4,24,384]{3,2,1,0:T(8,128)(2,1)S(1)}, u32[]{:S(2)}, u32[]{:S(2)}) %collective-permute-start.14) | collective-permute-done | bytes 147488 | tf_op jit(solution)/shard_map/ppermute | solution.py:13
  173.1 2.1 %fusion.12 = bf16[1,2,16,24,384]{4,3,2,1,0:T(8,128)(2,1)} fusion(f32[16,24]{1,0:T(8,128)S(1)} %get-tuple-element.154, f32[16,24]{1,0:T(8,128)S(1)} %get-tuple-element.155, bf16[2,4,4,384]{3,2,1,0:T(4,128)(2,1)S(1)} %collective-permute-done.15, f32[16]{0:T(128)S(1)} %get-tuple-element.179, bf16[2,4,24,384]{3,2,1,0:T(8,128)(2,1)S(1)} %collective-permute-done.14, ...), kind=kLoop, calls=%fused_computation.55 | loop fusion | flops 7962624 | bytes 1777472 | tf_op jit(solution)/shard_map/broadcast_in_dim | solution.py:155
  (78 shorter events, 11.2 us)
Async XLA Ops:
  6.5 42.7 %all-gather.2.cloned.1.call-start = ((), (), s32[]{:S(2)}) async-start(), calls=%async_computation | async-start | bytes 2949120 | tf_op jit(solution)/shard_map/all_gather | solution.py:124
  28.8 22.2 %copy-start = (bf16[1,2,16,24,384]{4,3,2,1,0:T(8,128)(2,1)S(1)}, bf16[1,2,16,24,384]{4,3,2,1,0:T(8,128)(2,1)}, u32[]{:S(2)}) copy-start(bf16[1,2,16,24,384]{4,3,2,1,0:T(8,128)(2,1)} %param.22) | copy-start | bytes 1769476
  51.3 14.7 %collective-permute-start.1 = (bf16[4,4,24,384]{3,2,1,0:T(8,128)(2,1)S(1)}, bf16[4,4,24,384]{3,2,1,0:T(8,128)(2,1)S(1)}, u32[]{:S(2)}, u32[]{:S(2)}) collective-permute-start(bf16[4,4,24,384]{3,2,1,0:T(8,128)(2,1)S(1)} %get-tuple-element.150), channel_id=1, source_target_pairs={{0,4},{2,6},{1,5},{3,7},{8,12},{10,14},{9,13},{11,15},{16,20},{18,... | collective-permute-start | bytes 884744 | tf_op jit(solution)/shard_map/ppermute | solution.py:13
  56.4 8.3 %collective-permute-start = (bf16[4,4,4,384]{3,2,1,0:T(4,128)(2,1)S(1)}, bf16[4,4,4,384]{3,2,1,0:T(4,128)(2,1)S(1)}, u32[]{:S(2)}, u32[]{:S(2)}) collective-permute-start(bf16[4,4,4,384]{3,2,1,0:T(4,128)(2,1)S(1)} %get-tuple-element.146), channel_id=1, source_target_pairs={{0,6},{1,7},{8,14},{9,15},{16,22},{17,23},{24,30},{25,31}} | collective-permute-start | bytes 147464 | tf_op jit(solution)/shard_map/ppermute | solution.py:13
  58.8 37.5 %collective-permute-start.7 = (bf16[4,4,4,384]{3,2,1,0:T(4,128)(2,1)}, bf16[4,4,4,384]{3,2,1,0:T(4,128)(2,1)}, u32[]{:S(2)}, u32[]{:S(2)}) collective-permute-start(bf16[4,4,4,384]{3,2,1,0:T(4,128)(2,1)} %get-tuple-element.145), channel_id=1, source_target_pairs={{6,0},{7,1},{14,8},{15,9},{22,16},{23,17},{30,24},{31,25}} | collective-permute-start | bytes 147464 | tf_op jit(solution)/shard_map/ppermute | solution.py:13
  60.1 17.4 %collective-permute-start.2 = (bf16[4,4,4,384]{3,2,1,0:T(4,128)(2,1)}, bf16[4,4,4,384]{3,2,1,0:T(4,128)(2,1)}, u32[]{:S(2)}, u32[]{:S(2)}) collective-permute-start(bf16[4,4,4,384]{3,2,1,0:T(4,128)(2,1)} %get-tuple-element.147), channel_id=1, source_target_pairs={{0,2},{2,4},{4,6},{1,3},{3,5},{5,7},{8,10},{10,12},{12,14},{9,11},... | collective-permute-start | bytes 147464 | tf_op jit(solution)/shard_map/ppermute | solution.py:13
  62.5 23.3 %collective-permute-start.5 = (bf16[4,4,4,384]{3,2,1,0:T(4,128)(2,1)}, bf16[4,4,4,384]{3,2,1,0:T(4,128)(2,1)}, u32[]{:S(2)}, u32[]{:S(2)}) collective-permute-start(bf16[4,4,4,384]{3,2,1,0:T(4,128)(2,1)} %get-tuple-element.148), channel_id=1, source_target_pairs={{2,0},{4,2},{6,4},{3,1},{5,3},{7,5},{10,8},{12,10},{14,12},{11,9},... | collective-permute-start | bytes 147464 | tf_op jit(solution)/shard_map/ppermute | solution.py:13
  64.6 21.0 %collective-permute-start.4 = (bf16[4,16,4,384]{3,2,1,0:T(4,128)(2,1)S(1)}, bf16[4,16,4,384]{3,2,1,0:T(4,128)(2,1)S(1)}, u32[]{:S(2)}, u32[]{:S(2)}) collective-permute-start(bf16[4,16,4,384]{3,2,1,0:T(4,128)(2,1)S(1)} %get-tuple-element.151), channel_id=1, source_target_pairs={{2,0},{4,2},{6,4},{3,1},{5,3},{7,5},{10,8},{12,10},{14,12},{11,9},... | collective-permute-start | bytes 589832 | tf_op jit(solution)/shard_map/ppermute | solution.py:13
  66.0 18.6 %collective-permute-start.3 = (bf16[4,16,4,384]{3,2,1,0:T(4,128)(2,1)S(1)}, bf16[4,16,4,384]{3,2,1,0:T(4,128)(2,1)}, u32[]{:S(2)}, u32[]{:S(2)}) collective-permute-start(bf16[4,16,4,384]{3,2,1,0:T(4,128)(2,1)S(1)} %get-tuple-element.152), channel_id=1, source_target_pairs={{0,2},{2,4},{4,6},{1,3},{3,5},{5,7},{8,10},{10,12},{12,14},{9,11},... | collective-permute-start | bytes 589832 | tf_op jit(solution)/shard_map/ppermute | solution.py:13
  77.5 17.6 %collective-permute-start.6 = (bf16[4,4,24,384]{3,2,1,0:T(8,128)(2,1)S(1)}, bf16[4,4,24,384]{3,2,1,0:T(8,128)(2,1)S(1)}, u32[]{:S(2)}, u32[]{:S(2)}) collective-permute-start(bf16[4,4,24,384]{3,2,1,0:T(8,128)(2,1)S(1)} %get-tuple-element.149), channel_id=1, source_target_pairs={{4,0},{6,2},{5,1},{7,3},{12,8},{14,10},{13,9},{15,11},{20,16},{22,... | collective-permute-start | bytes 884744 | tf_op jit(solution)/shard_map/ppermute | solution.py:13
  112.2 3.4 %copy-start.14 = (bf16[1,1,3,384,384]{4,3,2,1,0:T(8,128)(2,1)S(1)}, bf16[1,1,3,384,384]{4,3,2,1,0:T(8,128)(2,1)}, u32[]{:S(2)}) copy-start(bf16[1,1,3,384,384]{4,3,2,1,0:T(8,128)(2,1)} %get-tuple-element.108) | copy-start | bytes 2654212
  115.7 2.1 %copy-start.13 = (bf16[1,1,3,384,384]{4,3,2,1,0:T(8,128)(2,1)S(1)}, bf16[1,1,3,384,384]{4,3,2,1,0:T(8,128)(2,1)}, u32[]{:S(2)}) copy-start(bf16[1,1,3,384,384]{4,3,2,1,0:T(8,128)(2,1)} %get-tuple-element.107) | copy-start | bytes 2654212
  117.8 3.7 %copy-start.2 = (bf16[2,24,32,384]{3,2,1,0:T(8,128)(2,1)S(1)}, bf16[2,24,32,384]{3,2,1,0:T(8,128)(2,1)}, u32[]{:S(2)}) copy-start(bf16[2,24,32,384]{3,2,1,0:T(8,128)(2,1)} %get-tuple-element.110) | copy-start | bytes 3538948
  117.8 3.7 %copy-start.3 = (bf16[2,24,32,384]{3,2,1,0:T(8,128)(2,1)S(1)}, bf16[2,24,32,384]{3,2,1,0:T(8,128)(2,1)}, u32[]{:S(2)}) copy-start(bf16[2,24,32,384]{3,2,1,0:T(8,128)(2,1)} %get-tuple-element.111) | copy-start | bytes 3538948
  117.8 3.7 %copy-start.4 = (bf16[2,24,32,384]{3,2,1,0:T(8,128)(2,1)S(1)}, bf16[2,24,32,384]{3,2,1,0:T(8,128)(2,1)}, u32[]{:S(2)}) copy-start(bf16[2,24,32,384]{3,2,1,0:T(8,128)(2,1)} %get-tuple-element.112) | copy-start | bytes 3538948
  121.5 1.9 %copy-start.1 = (bf16[2,24,32,384]{3,2,1,0:T(8,128)(2,1)S(1)}, bf16[2,24,32,384]{3,2,1,0:T(8,128)(2,1)}, u32[]{:S(2)}) copy-start(bf16[2,24,32,384]{3,2,1,0:T(8,128)(2,1)} %get-tuple-element.128) | copy-start | bytes 3538948
  123.4 1.2 copy-start.12
  124.6 4.0 %copy-start.11 = (bf16[1,1,3,384,384]{4,3,2,1,0:T(8,128)(2,1)S(1)}, bf16[1,1,3,384,384]{4,3,2,1,0:T(8,128)(2,1)}, u32[]{:S(2)}) copy-start(bf16[1,1,3,384,384]{4,3,2,1,0:T(8,128)(2,1)} %get-tuple-element.105) | copy-start | bytes 2654212
  130.7 1.2 copy-start.10
  131.9 2.2 %copy-start.9 = (bf16[1,1,3,384,384]{4,3,2,1,0:T(8,128)(2,1)S(1)}, bf16[1,1,3,384,384]{4,3,2,1,0:T(8,128)(2,1)}, u32[]{:S(2)}) copy-start(bf16[1,1,3,384,384]{4,3,2,1,0:T(8,128)(2,1)} %get-tuple-element.103) | copy-start | bytes 2654212
  136.2 1.2 copy-start.8
  137.4 2.2 %copy-start.7 = (bf16[1,1,3,384,384]{4,3,2,1,0:T(8,128)(2,1)S(1)}, bf16[1,1,3,384,384]{4,3,2,1,0:T(8,128)(2,1)}, u32[]{:S(2)}) copy-start(bf16[1,1,3,384,384]{4,3,2,1,0:T(8,128)(2,1)} %get-tuple-element.109) | copy-start | bytes 2654212
  139.6 2.1 %copy-start.5 = (bf16[2,24,32,1152]{3,2,1,0:T(8,128)(2,1)S(1)}, bf16[2,24,32,1152]{3,2,1,0:T(8,128)(2,1)}, u32[]{:S(2)}) copy-start(bf16[2,24,32,1152]{3,2,1,0:T(8,128)(2,1)} %pad_maximum_fusion.8) | copy-start | bytes 10616836
  139.6 2.2 %copy-start.6 = (bf16[1,1,3,384,384]{4,3,2,1,0:T(8,128)(2,1)S(1)}, bf16[1,1,3,384,384]{4,3,2,1,0:T(8,128)(2,1)}, u32[]{:S(2)}) copy-start(bf16[1,1,3,384,384]{4,3,2,1,0:T(8,128)(2,1)} %get-tuple-element.101) | copy-start | bytes 2654212
  141.8 2.1 %copy-start.16 = (f32[384]{0:T(512)S(1)}, f32[384]{0:T(512)}, u32[]{:S(2)}) copy-start(f32[384]{0:T(512)} %param.27) | copy-start | bytes 4612
  143.9 20.5 %copy-start.15 = (f32[24]{0:T(128)S(1)}, f32[24]{0:T(128)}, u32[]{:S(2)}) copy-start(f32[24]{0:T(128)} %get-tuple-element.182) | copy-start | bytes 292
  144.4 10.5 %collective-permute-start.8 = (bf16[2,4,4,384]{3,2,1,0:T(4,128)(2,1)S(1)}, bf16[2,4,4,384]{3,2,1,0:T(4,128)(2,1)S(1)}, u32[]{:S(2)}, u32[]{:S(2)}) collective-permute-start(bf16[2,4,4,384]{3,2,1,0:T(4,128)(2,1)S(1)} %get-tuple-element.137), channel_id=1, source_target_pairs={{0,6},{1,7},{8,14},{9,15},{16,22},{17,23},{24,30},{25,31}} | collective-permute-start | bytes 73736 | tf_op jit(solution)/shard_map/ppermute | solution.py:13
  145.7 10.5 %collective-permute-start.15 = (bf16[2,4,4,384]{3,2,1,0:T(4,128)(2,1)S(1)}, bf16[2,4,4,384]{3,2,1,0:T(4,128)(2,1)S(1)}, u32[]{:S(2)}, u32[]{:S(2)}) collective-permute-start(bf16[2,4,4,384]{3,2,1,0:T(4,128)(2,1)S(1)} %get-tuple-element.138), channel_id=1, source_target_pairs={{6,0},{7,1},{14,8},{15,9},{22,16},{23,17},{30,24},{31,25}} | collective-permute-start | bytes 73736 | tf_op jit(solution)/shard_map/ppermute | solution.py:13
  147.0 16.1 %collective-permute-start.13 = (bf16[2,4,4,384]{3,2,1,0:T(4,128)(2,1)S(1)}, bf16[2,4,4,384]{3,2,1,0:T(4,128)(2,1)S(1)}, u32[]{:S(2)}, u32[]{:S(2)}) collective-permute-start(bf16[2,4,4,384]{3,2,1,0:T(4,128)(2,1)S(1)} %get-tuple-element.139), channel_id=1, source_target_pairs={{2,0},{4,2},{6,4},{3,1},{5,3},{7,5},{10,8},{12,10},{14,12},{11,9},... | collective-permute-start | bytes 73736 | tf_op jit(solution)/shard_map/ppermute | solution.py:13
  148.4 16.1 %collective-permute-start.10 = (bf16[2,4,4,384]{3,2,1,0:T(4,128)(2,1)S(1)}, bf16[2,4,4,384]{3,2,1,0:T(4,128)(2,1)S(1)}, u32[]{:S(2)}, u32[]{:S(2)}) collective-permute-start(bf16[2,4,4,384]{3,2,1,0:T(4,128)(2,1)S(1)} %get-tuple-element.140), channel_id=1, source_target_pairs={{0,2},{2,4},{4,6},{1,3},{3,5},{5,7},{8,10},{10,12},{12,14},{9,11},... | collective-permute-start | bytes 73736 | tf_op jit(solution)/shard_map/ppermute | solution.py:13
  152.9 11.6 %collective-permute-start.11 = (bf16[2,16,4,384]{3,2,1,0:T(4,128)(2,1)S(1)}, bf16[2,16,4,384]{3,2,1,0:T(4,128)(2,1)S(1)}, u32[]{:S(2)}, u32[]{:S(2)}) collective-permute-start(bf16[2,16,4,384]{3,2,1,0:T(4,128)(2,1)S(1)} %get-tuple-element.143), channel_id=1, source_target_pairs={{0,2},{2,4},{4,6},{1,3},{3,5},{5,7},{8,10},{10,12},{12,14},{9,11},... | collective-permute-start | bytes 294920 | tf_op jit(solution)/shard_map/ppermute | solution.py:13
  154.9 9.6 %collective-permute-start.12 = (bf16[2,16,4,384]{3,2,1,0:T(4,128)(2,1)S(1)}, bf16[2,16,4,384]{3,2,1,0:T(4,128)(2,1)S(1)}, u32[]{:S(2)}, u32[]{:S(2)}) collective-permute-start(bf16[2,16,4,384]{3,2,1,0:T(4,128)(2,1)S(1)} %get-tuple-element.144), channel_id=1, source_target_pairs={{2,0},{4,2},{6,4},{3,1},{5,3},{7,5},{10,8},{12,10},{14,12},{11,9},... | collective-permute-start | bytes 294920 | tf_op jit(solution)/shard_map/ppermute | solution.py:13
  156.2 9.6 %collective-permute-start.9 = (bf16[2,4,24,384]{3,2,1,0:T(8,128)(2,1)S(1)}, bf16[2,4,24,384]{3,2,1,0:T(8,128)(2,1)S(1)}, u32[]{:S(2)}, u32[]{:S(2)}) collective-permute-start(bf16[2,4,24,384]{3,2,1,0:T(8,128)(2,1)S(1)} %get-tuple-element.141), channel_id=1, source_target_pairs={{0,4},{2,6},{1,5},{3,7},{8,12},{10,14},{9,13},{11,15},{16,20},{18,... | collective-permute-start | bytes 442376 | tf_op jit(solution)/shard_map/ppermute | solution.py:13
  163.1 10.0 %collective-permute-start.14 = (bf16[2,4,24,384]{3,2,1,0:T(8,128)(2,1)S(1)}, bf16[2,4,24,384]{3,2,1,0:T(8,128)(2,1)S(1)}, u32[]{:S(2)}, u32[]{:S(2)}) collective-permute-start(bf16[2,4,24,384]{3,2,1,0:T(8,128)(2,1)S(1)} %get-tuple-element.142), channel_id=1, source_target_pairs={{4,0},{6,2},{5,1},{7,3},{12,8},{14,10},{13,9},{15,11},{20,16},{22,... | collective-permute-start | bytes 442376 | tf_op jit(solution)/shard_map/ppermute | solution.py:13
Sparse Core Ops, SparseCore 0:
  9.2 40.0 all-gather.1
where the time goes:
time: 183 us; the launch traced here: 182 us
  starting transfers between devices  41.4 us (23%)
  waiting for transfers between devices  38.2 us (21%)
  local copies, waits for them, and re-layouts  31.3 us (17%)
  other arithmetic  26.4 us (14%)
  matrix products  22.5 us (12%)
  between operations  22.2 us (12%)
    ppermute x16, starting transfers between devices, passed_along(): return lax.ppermute(shard, axis, pairs)  41.4 us
    dot_general x9, matrix products, convolve(): jnp.dot(flattened, kernel[tap_time, tap_row].reshape(3 * channels, -1), p...  22.5 us
    all_gather x1, waiting for transfers between devices, local(): pieces = lax.all_gather(own_block[None], 'group', axis=0, tiled=True)  20.4 us
    ppermute x16, waiting for transfers between devices, passed_along(): return lax.ppermute(shard, axis, pairs)  17.1 us
    slice x2, local copies, waits for them, and re-layouts, convolve(): window[:, :, tap_col:tap_col + col_count]  10.8 us
    scatter x8, local copies, waits for them, and re-layouts, gather_rims(): result.at[:, row_dest:row_dest + row_len, col_dest:col_dest + col_len]  8.67 us
    another operation x6, other arithmetic  8.1 us
    concatenate x5, other arithmetic, convolve(): jnp.concatenate([window[:, :, tap_col:tap_col + col_count] for tap_col in...  8 us
  transfers between devices with their start and end apart: 17, of which 4 were waited for; matrix products, arithmetic and copies ran while one was open for 16% of the time, Pallas kernels for 0%

commit v1 on v0

v1 whole, which is shorter than its diff:
```python
import functools
import itertools

import jax
import jax.numpy as jnp
from jax import lax
from jax.experimental import pallas as pl
from jax.experimental.pallas import tpu as pltpu
from jax.sharding import PartitionSpec as P

GRID_R = 2
MESH = pl.DeviceIdType.MESH
DIRS = ((-1, 0), (1, 0), (0, -1), (0, 1), (-1, -1), (-1, 1), (1, -1), (1, 1))


def activate(values, gain):
    widened = values.astype(jnp.float32)
    inv_norm = lax.rsqrt(jnp.mean(widened * widened, axis=-1, keepdims=True) + 1e-06)
    u = widened * inv_norm * gain
    return u / (1.0 + jnp.exp(-u))


def table(index, values):
    out = jnp.int32(values[0])
    for k in range(1, len(values)):
        out = jnp.where(index == k, jnp.int32(values[k]), out)
    return out


def body(order, n_tile, slot_ref, margin_ref, x_ref, gain_ref, bias_ref, w_hbm, out_ref,
         prev, rows_in, cols_in, corners_in, cols_out, w, act, z, acc,
         send_small, recv_small, send_big, recv_big, w_sem):
    frames, core_h, core_w, channels = x_ref.shape
    n_group = len(order)
    grid_cols = n_tile // GRID_R
    group = lax.axis_index("group")
    tile = lax.axis_index("tile")
    tile_row = tile // grid_cols
    tile_col = tile % grid_cols
    following = [0] * n_group
    preceding = [0] * n_group
    for k in range(n_group):
        following[order[k]] = order[(k + 1) % n_group]
        preceding[order[(k + 1) % n_group]] = order[k]
    nxt = table(group, following)
    before = table(group, preceding)

    for a in (2, 1, 0):
        pltpu.make_async_copy(w_hbm.at[a], w.at[a], w_sem.at[a]).start()

    def present(step_r, step_c):
        ok = None
        for at, step, most in ((tile_row, step_r, GRID_R), (tile_col, step_c, grid_cols)):
            if step == 0:
                continue
            here = (at > 0) if step < 0 else (at < most - 1)
            ok = here if ok is None else jnp.logical_and(ok, here)
        return ok

    barrier = pltpu.get_barrier_semaphore()
    greeted = jnp.int32(2)
    for peer in (nxt, before):
        pl.semaphore_signal(barrier, inc=1, device_id={"group": peer}, device_id_type=MESH)
    for step_r, step_c in DIRS:
        ok = present(step_r, step_c)
        greeted = greeted + 3 * ok.astype(jnp.int32)

        @pl.when(ok)
        def _():
            other = tile + step_r * grid_cols + step_c
            for peer in (group, nxt, before):
                pl.semaphore_signal(barrier, inc=1, device_id={"group": peer, "tile": other},
                                    device_id_type=MESH)

    for f in range(frames):
        edge = x_ref[f].astype(jnp.float32)
        cols_out[0, f] = edge[:, 0, :].astype(jnp.bfloat16)
        cols_out[1, f] = edge[:, core_w - 1, :].astype(jnp.bfloat16)

    pl.semaphore_wait(barrier, greeted)

    def rim_copy(kind, n):
        step_r, step_c = DIRS[n]
        peer = nxt if kind else group
        other = tile + step_r * grid_cols + step_c
        if step_c == 0:
            src = x_ref.at[:, 0 if step_r < 0 else core_h - 1]
            dst = rows_in.at[kind, 1 if step_r < 0 else 0]
        elif step_r == 0:
            src = cols_out.at[0 if step_c < 0 else 1]
            dst = cols_in.at[kind, 1 if step_c < 0 else 0]
        else:
            first = 0 if step_c < 0 else core_w - 8
            src = x_ref.at[:, 0 if step_r < 0 else core_h - 1, pl.ds(first, 8)]
            dst = corners_in.at[kind, 1 if step_r < 0 else 0, 1 if step_c < 0 else 0]
        return pltpu.make_async_remote_copy(
            src_ref=src, dst_ref=dst, send_sem=send_small.at[kind, n], recv_sem=recv_small.at[kind, n],
            device_id={"group": peer, "tile": other}, device_id_type=MESH)

    def block_copy(f):
        return pltpu.make_async_remote_copy(
            src_ref=x_ref.at[f], dst_ref=prev.at[f], send_sem=send_big.at[f], recv_sem=recv_big.at[f],
            device_id={"group": nxt}, device_id_type=MESH)

    for kind in (0, 1):
        for n, (step_r, step_c) in enumerate(DIRS):
            @pl.when(present(step_r, step_c))
            def _():
                rim_copy(kind, n).start()
    for f in (1, 0):
        block_copy(f).start()

    gain = gain_ref[...]
    pitch = core_w + 16
    left, right, up, down = [margin_ref[0, k] for k in range(4)]
    not_first = jnp.full((1, channels), slot_ref[group] > 0)

    def kept(m):
        m_f = jnp.full((core_h, channels), m, jnp.int32).astype(jnp.float32)
        return (m_f + 1.0) / (m_f + 2.0)

    row_at = lax.broadcasted_iota(jnp.int32, (core_h, channels), 0)
    alpha = [jnp.where(row_at == core_h - down, kept(down), 1.0), None,
             jnp.where(row_at == up - 1, kept(up), 1.0)]
    beta_left = kept(left)
    beta_right = kept(right)

    def build(kind, f, source, slot):
        def gated(v):
            return jnp.where(not_first, v, 0.0) if kind else v

        lanes = channels // 128

        def store(at, v):
            for c in range(lanes):
                act[slot, c, at] = v[:, c * 128:(c + 1) * 128]

        def fetch(at):
            return jnp.concatenate([act[slot, c, at] for c in range(lanes)], axis=-1)

        store(pl.ds(0, pitch), jnp.zeros((pitch, channels), jnp.float32))
        store(pl.ds((core_h + 1) * pitch, pitch), jnp.zeros((pitch, channels), jnp.float32))
        store(pl.ds(pitch + 7, core_h, stride=pitch), jnp.zeros((core_h, channels), jnp.float32))
        store(pl.ds(pitch + 8 + core_w, core_h, stride=pitch), jnp.zeros((core_h, channels), jnp.float32))

        def one_row(i, carry):
            at = pl.multiple_of((i + 1) * pitch + 8, 8)
            store(pl.ds(at, core_w), gated(activate(source[f, i], gain)))
            return carry
        lax.fori_loop(0, core_h, one_row, 0, unroll=2)
        for n, (step_r, step_c) in enumerate(DIRS):
            @pl.when(present(step_r, step_c))
            def _():
                vertical = (core_h + 1) * pitch if step_r > 0 else 0
                if step_c == 0:
                    store(pl.ds(vertical + 8, core_w), gated(activate(rows_in[kind, 1 if step_r > 0 else 0, f], gain)))
                elif step_r == 0:
                    start = pitch + (8 + core_w if step_c > 0 else 7)
                    store(pl.ds(start, core_h, stride=pitch),
                          gated(activate(cols_in[kind, 1 if step_c > 0 else 0, f], gain)))
                else:
                    v = gated(activate(corners_in[kind, 1 if step_r > 0 else 0, 1 if step_c > 0 else 0, f], gain))
                    at = vertical + (8 + core_w if step_c > 0 else 7)
                    store(pl.ds(at, 1), v[0:1] if step_c > 0 else v[7:8])

        def one_col(j, carry):
            for b in range(3):
                for e in range(3):
                    v = fetch(pl.ds(b * pitch + 7 + j + e, core_h, stride=pitch))
                    if alpha[b] is not None:
                        v = v * alpha[b]
                    if e == 2:
                        v = jnp.where(j == left - 1, v * beta_left, v)
                    if e == 0:
                        v = jnp.where(j == core_w - right, v * beta_right, v)
                    z[slot, b, pl.ds(pl.multiple_of(j * core_h, core_h), core_h),
                      e * channels:(e + 1) * channels] = v.astype(jnp.bfloat16)
            return carry
        lax.fori_loop(0, core_w, one_col, 0)

    def wait_rims(kind):
        for n, (step_r, step_c) in enumerate(DIRS):
            m = DIRS.index((-step_r, -step_c))

            @pl.when(present(step_r, step_c))
            def _():
                rim_copy(kind, m).wait_recv()

    def wait_w(a):
        pltpu.make_async_copy(w_hbm.at[a], w.at[a], w_sem.at[a]).wait()

    wait_rims(0)
    build(0, 0, x_ref, 0)
    build(0, 1, x_ref, 1)
    wait_w(2)
    wait_w(1)
    acc[...] = jnp.zeros(acc.shape, jnp.float32)

    def both(slot, a_first, a_second):
        def step(b, carry):
            rhs = jnp.concatenate([w[a_first, b], w[a_second, b]], axis=-1)
            acc[...] += jnp.dot(z[slot, b], rhs, preferred_element_type=jnp.float32)
            return carry
        lax.fori_loop(0, 3, step, 0)

    def single(slot, a, s):
        cols = slice(s * channels, (s + 1) * channels)

        def step(b, carry):
            acc[:, cols] += jnp.dot(z[slot, b], w[a, b], preferred_element_type=jnp.float32)
            return carry
        lax.fori_loop(0, 3, step, 0)

    both(0, 2, 1)
    single(1, 2, 1)
    wait_w(0)
    wait_rims(1)
    block_copy(1).wait_recv()
    build(1, 1, prev, 1)
    both(1, 1, 0)
    block_copy(0).wait_recv()
    build(1, 0, prev, 0)
    single(0, 0, 0)

    bias = bias_ref[...]
    for s in range(frames):
        for c in range(channels // 128):
            first = s * channels + c * 128
            act[s, c, pl.ds(0, core_h * core_w)] = acc[:, first:first + 128]

        def put(i, carry):
            v = jnp.concatenate([act[s, c, pl.ds(i, core_w, stride=core_h)] for c in range(channels // 128)], axis=-1)
            out_ref[s, i] = (v + bias).astype(out_ref.dtype)
            return carry
        lax.fori_loop(0, core_h, put, 0)

    for kind in (0, 1):
        for n, (step_r, step_c) in enumerate(DIRS):
            @pl.when(present(step_r, step_c))
            def _():
                rim_copy(kind, n).wait_send()
    for f in (1, 0):
        block_copy(f).wait_send()


def local(orders, n_tile, features, group_slot, margins, norm_gain, kernel, conv_bias):
    x = features[0]
    frames, core_h, core_w, channels = x.shape
    n_group = group_slot.shape[0]
    weights = kernel.reshape(3, 3, 3 * channels, channels)
    rel = lax.rem(group_slot - group_slot[0] + n_group, n_group)
    branch = jnp.int32(0)
    for k, order in enumerate(orders):
        hit = jnp.bool_(True)
        for position, device in enumerate(order):
            hit = hit & (rel[device] == position)
        branch = branch + jnp.where(hit, k, 0)

    pitch = core_w + 16
    vmem = pl.BlockSpec(memory_space=pltpu.VMEM)
    smem = pl.BlockSpec(memory_space=pltpu.SMEM)

    def call(k):
        def run(slot, margin, xx, gain, bias, w):
            return pl.pallas_call(
                functools.partial(body, orders[k], n_tile),
                out_shape=jax.ShapeDtypeStruct(x.shape, jnp.bfloat16),
                in_specs=[smem, smem, vmem, vmem, vmem, pl.BlockSpec(memory_space=pl.ANY)],
                out_specs=vmem,
                scratch_shapes=[
                    pltpu.VMEM((frames, core_h, core_w, channels), jnp.bfloat16),
                    pltpu.VMEM((2, 2, frames, core_w, channels), jnp.bfloat16),
                    pltpu.VMEM((2, 2, frames, core_h, channels), jnp.bfloat16),
                    pltpu.VMEM((2, 2, 2, frames, 8, channels), jnp.bfloat16),
                    pltpu.VMEM((2, frames, core_h, channels), jnp.bfloat16),
                    pltpu.VMEM((3, 3, 3 * channels, channels), jnp.bfloat16),
                    pltpu.VMEM((2, channels // 128, (core_h + 2) * pitch, 128), jnp.float32),
                    pltpu.VMEM((2, 3, core_h * core_w, 3 * channels), jnp.bfloat16),
                    pltpu.VMEM((core_h * core_w, 2 * channels), jnp.float32),
                    pltpu.SemaphoreType.DMA((2, 8)),
                    pltpu.SemaphoreType.DMA((2, 8)),
                    pltpu.SemaphoreType.DMA((2,)),
                    pltpu.SemaphoreType.DMA((2,)),
                    pltpu.SemaphoreType.DMA((3,)),
                ],
                compiler_params=pltpu.CompilerParams(collective_id=k, has_side_effects=True),
                name="conv_order_%d" % k,
            )(slot, margin, xx, gain, bias, w)
        return run

    out = lax.switch(branch, [call(k) for k in range(len(orders))], group_slot, margins, x,
                     norm_gain[None], conv_bias[None], weights)
    return out[None]


def solution(mesh):
    n_group = mesh.shape["group"]
    n_tile = mesh.shape["tile"]
    orders = [(0,) + rest for rest in itertools.permutations(range(1, n_group))]
    return jax.shard_map(
        functools.partial(local, orders, n_tile),
        mesh=mesh,
        in_specs=(
            P(("video", "tile"), "group", None, None, None),
            P(),
            P("tile", None),
            P(),
            P(),
            P(),
        ),
        out_specs=P(("video", "tile"), "group", None, None, None),
        check_vma=False,
    )
```

time: 183 us -> 43.5 us (0.24)
  starting transfers between devices: 41.4 us -> 0 us
  waiting for transfers between devices: 38.2 us -> 0 us
  Pallas kernels: 0 us -> 32.5 us
  local copies, waits for them, and re-layouts: 31.3 us -> 2.84 us
  other arithmetic: 26.4 us -> 1.31 us
  matrix products: 22.5 us -> 0 us
  between operations: 22.2 us -> 6.35 us
    ppermute x16 -> x0, starting transfers between devices: 41.4 us -> none  [passed_along(): return lax.ppermute(shard, axis, pairs)]
    pallas_call x0 -> x1, Pallas kernels: none -> 32.5 us  [run(): pl.pallas_call(functools.partial(body, orders[k], n_tile), out_shape=jax....]
    dot_general x9 -> x0, matrix products: 22.5 us -> none  [convolve(): jnp.dot(flattened, kernel[tap_time, tap_row].reshape(3 * channels, -1), p...]
    all_gather x1 -> x0, waiting for transfers between devices: 20.4 us -> none  [local(): pieces = lax.all_gather(own_block[None], 'group', axis=0, tiled=True)]
    slice x7 -> x1, local copies, waits for them, and re-layouts: 18.1 us -> 0.66 us  [local(): hit = hit & (rel[device] == position)]
    ppermute x16 -> x0, waiting for transfers between devices: 17.1 us -> none  [passed_along(): return lax.ppermute(shard, axis, pairs)]
    concatenate x9 -> x0, other arithmetic: 9.16 us -> none  [the longest x5 8 us: convolve(): jnp.concatenate([window[:, :, tap_col:tap_col + col_count] for tap_col in...]
    scatter x8 -> x0, local copies, waits for them, and re-layouts: 8.67 us -> none  [gather_rims(): result.at[:, row_dest:row_dest + row_len, col_dest:col_dest + col_len]]
  transfers between devices with their start and end apart: 17 -> 0, of which waited for: 4 -> 0; matrix products, arithmetic and copies ran while one was open for 16% -> 0% of each run, Pallas kernels for 0% -> 0%
where the time goes in v1:
time: 43.5 us; the launch traced here: 43.2 us
  Pallas kernels  32.5 us (75%)
  between operations  6.35 us (15%)
  local copies, waits for them, and re-layouts  2.84 us (7%)
  other arithmetic  1.31 us (3%)
    pallas_call x1, Pallas kernels, run(): pl.pallas_call(functools.partial(body, orders[k], n_tile), out_shape=jax....  32.5 us
    rem x1, other arithmetic, local(): rel = lax.rem(group_slot - group_slot[0] + n_group, n_group)  1.31 us

profile of v1, /device:TPU:0, one launch (start us, length us, event | category | flops | bytes accessed | tf_op | source)
XLA Modules:
  0.0 43.2 jit_solution(1504187129336544054)
XLA Ops:
  0.0 1.3 %compare_select_fusion = s32[4]{0:T(128)S(1)} fusion(s32[4]{0:T(128)} %param.13, s32[]{:T(128)} %bitcast.29), kind=kLoop, calls=%fused_computation | loop fusion | flops 32 | bytes 36 | tf_op jit(solution)/shard_map/rem | solution.py:251
  1.3 0.7 %broadcast_in_dim.25 = f32[1,384]{1,0:T(1,128)S(1)} reshape(f32[384]{0:T(512)} %param.15) | data formatting | bytes 3072 | tf_op jit(solution)/shard_map/broadcast_in_dim | solution.py:292
  2.0 0.7 %broadcast_in_dim.26 = f32[1,384]{1,0:T(1,128)S(1)} reshape(f32[384]{0:T(512)} %param.17) | data formatting | bytes 3072 | tf_op jit(solution)/shard_map/broadcast_in_dim | solution.py:292
  2.7 0.7 %fusion.1 = (s32[1]{0:T(128)}, s32[1]{0:T(128)}, s32[1]{0:T(128)}, s32[1]{0:T(128)}) fusion(s32[4]{0:T(128)S(1)} %compare_select_fusion), kind=kLoop, calls=%fused_computation.3 | loop fusion | bytes 32 | tf_op jit(solution)/shard_map/slice | solution.py:256
  9.7 32.7 %conditional.1 = (bf16[1,2,16,24,384]{4,3,2,1,0:T(8,128)(2,1)S(1)}) conditional(s32[]{:T(128)} %bitcast.7, (s32[4]{0:T(128)}, s32[1,4]{1,0:T(1,128)}, bf16[2,16,24,384]{3,2,1,0:T(8,128)(2,1)}, f32[1,384]{1,0:T(1,128)S(1)}, f32[1,384]{1,0:T(1,128)S(1)}, /*index=5*/bf16[3,3,1152,384]{3,2,1,0:T(8,128)(2,1)}) %tuple.51, ...), branch_computations={%region_0.1_spmd, %region_1.2_spmd, %region_2.3_spmd, %region_3.4_... | conditional | bytes 8 | solution.py:291
  9.9 32.5 %conv_order_4.1 = bf16[2,16,24,384]{3,2,1,0:T(8,128)(2,1)S(1)} custom-call(s32[4]{0:T(128)} %get-tuple-element.109.slot_ref, s32[1,4]{1,0:T(1,128)} %get-tuple-element.110.margin_ref, bf16[2,16,24,384]{3,2,1,0:T(8,128)(2,1)} %get-tuple-element.111.x_ref, f32[1,384]{1,0:T(1,128)S(1)} %get-tuple-element.112.gain_ref, ...), custom_call_target="tpu_custom_call" | custom-call | tf_op jit(solution)/shard_map/cond/branch_4_fun/conv_order_4/pallas_call | solution.py:265
  42.4 0.8 %copy.20 = bf16[1,2,16,24,384]{4,3,2,1,0:T(8,128)(2,1)} copy(bf16[1,2,16,24,384]{4,3,2,1,0:T(8,128)(2,1)S(1)} %get-tuple-element.121) | data formatting | bytes 1179648

commit v2 on v1

--- a/solution.py
+++ b/solution.py
@@ -16,8 +16,8 @@
 def activate(values, gain):
     widened = values.astype(jnp.float32)
     inv_norm = lax.rsqrt(jnp.mean(widened * widened, axis=-1, keepdims=True) + 1e-06)
-    u = widened * inv_norm * gain
-    return u / (1.0 + jnp.exp(-u))
+    half = widened * inv_norm * (0.5 * gain)
+    return half + half * jnp.tanh(half)
 
 
 def table(index, values):
@@ -110,7 +110,7 @@
     for f in (1, 0):
         block_copy(f).start()
 
-    gain = gain_ref[...]
+    gain = gain_ref[...].reshape(1, channels)
     pitch = core_w + 16
     left, right, up, down = [margin_ref[0, k] for k in range(4)]
     not_first = jnp.full((1, channels), slot_ref[group] > 0)
@@ -144,10 +144,11 @@
         store(pl.ds(pitch + 8 + core_w, core_h, stride=pitch), jnp.zeros((core_h, channels), jnp.float32))
 
         def one_row(i, carry):
-            at = pl.multiple_of((i + 1) * pitch + 8, 8)
-            store(pl.ds(at, core_w), gated(activate(source[f, i], gain)))
-            return carry
-        lax.fori_loop(0, core_h, one_row, 0, unroll=2)
+            for k in range(4):
+                at = pl.multiple_of((4 * i + k + 1) * pitch + 8, 8)
+                store(pl.ds(at, core_w), gated(activate(source[f, 4 * i + k], gain)))
+            return carry
+        lax.fori_loop(0, core_h // 4, one_row, 0)
         for n, (step_r, step_c) in enumerate(DIRS):
             @pl.when(present(step_r, step_c))
             def _():
@@ -176,7 +177,7 @@
                     z[slot, b, pl.ds(pl.multiple_of(j * core_h, core_h), core_h),
                       e * channels:(e + 1) * channels] = v.astype(jnp.bfloat16)
             return carry
-        lax.fori_loop(0, core_w, one_col, 0)
+        lax.fori_loop(0, core_w, one_col, 0, unroll=2)
 
     def wait_rims(kind):
         for n, (step_r, step_c) in enumerate(DIRS):
@@ -222,7 +223,7 @@
     build(1, 0, prev, 0)
     single(0, 0, 0)
 
-    bias = bias_ref[...]
+    bias = bias_ref[...].reshape(1, channels)
     for s in range(frames):
         for c in range(channels // 128):
             first = s * channels + c * 128
@@ -243,18 +244,29 @@
         block_copy(f).wait_send()
 
 
-def local(orders, n_tile, features, group_slot, margins, norm_gain, kernel, conv_bias):
-    x = features[0]
-    frames, core_h, core_w, channels = x.shape
-    n_group = group_slot.shape[0]
-    weights = kernel.reshape(3, 3, 3 * channels, channels)
-    rel = lax.rem(group_slot - group_slot[0] + n_group, n_group)
+def pick(orders, slot_ref, branch_ref):
+    n_group = len(orders[0])
+    rel = [lax.rem(slot_ref[d] - slot_ref[0] + n_group, n_group) for d in range(n_group)]
     branch = jnp.int32(0)
     for k, order in enumerate(orders):
         hit = jnp.bool_(True)
         for position, device in enumerate(order):
-            hit = hit & (rel[device] == position)
-        branch = branch + jnp.where(hit, k, 0)
+            hit = jnp.logical_and(hit, rel[device] == position)
+        branch = jnp.where(hit, jnp.int32(k), branch)
+    branch_ref[0] = branch
+
+
+def local(orders, n_tile, features, group_slot, margins, norm_gain, kernel, conv_bias):
+    x = features[0]
+    frames, core_h, core_w, channels = x.shape
+    weights = kernel.reshape(3, 3, 3 * channels, channels)
+    branch = pl.pallas_call(
+        functools.partial(pick, orders),
+        out_shape=jax.ShapeDtypeStruct((1,), jnp.int32),
+        in_specs=[pl.BlockSpec(memory_space=pltpu.SMEM)],
+        out_specs=pl.BlockSpec(memory_space=pltpu.SMEM),
+        name="pick",
+    )(group_slot)[0]
 
     pitch = core_w + 16
     vmem = pl.BlockSpec(memory_space=pltpu.VMEM)
@@ -289,7 +301,7 @@
         return run
 
     out = lax.switch(branch, [call(k) for k in range(len(orders))], group_slot, margins, x,
-                     norm_gain[None], conv_bias[None], weights)
+                     norm_gain, conv_bias, weights)
     return out[None]
 
 

time: 43.5 us -> 32.2 us (0.74); the launches traced: 43.2 us -> 32.5 us
  between operations: 6.35 us -> 0.67 us
  local copies, waits for them, and re-layouts: 2.84 us -> 0.82 us
  Pallas kernels: 32.5 us -> 30.8 us
  other arithmetic: 1.31 us -> 0 us
    pallas_call x1, Pallas kernels: 32.5 us -> 29.6 us  [run(): pl.pallas_call(functools.partial(body, orders[k], n_tile), out_shape=jax....]
    broadcast_in_dim x2 -> x0, local copies, waits for them, and re-layouts: 1.37 us -> none  [the longest x1 0.68 us: local(): norm_gain[None]]
    rem x1 -> x0, other arithmetic: 1.31 us -> none  [local(): rel = lax.rem(group_slot - group_slot[0] + n_group, n_group)]
    pallas_call x0 -> x1, Pallas kernels: none -> 1.2 us  [local(): pl.pallas_call(functools.partial(pick, orders), out_shape=jax.ShapeDtypeS...]
    slice x1 -> x0, local copies, waits for them, and re-layouts: 0.66 us -> none  [local(): hit = hit & (rel[device] == position)]
where the time goes in v2:
time: 32.2 us; the launch traced here: 32.5 us
  Pallas kernels  30.8 us (96%)
  local copies, waits for them, and re-layouts  0.82 us (3%)
  between operations  0.67 us (2%)
    pallas_call x1, Pallas kernels, run(): pl.pallas_call(functools.partial(body, orders[k], n_tile), out_shape=jax....  29.6 us
    pallas_call x1, Pallas kernels, local(): pl.pallas_call(functools.partial(pick, orders), out_shape=jax.ShapeDtypeS...  1.2 us
    unnamed x1, local copies, waits for them, and re-layouts  0.82 us

profile of v2, /device:TPU:0, one launch (start us, length us, event | category | flops | bytes accessed | tf_op | source)
XLA Modules:
  0.0 32.5 jit_solution(6112393803406512729)
XLA Ops:
  0.0 1.2 %pick.1 = s32[1]{0:T(128)} custom-call(s32[4]{0:T(128)} %slot_ref.1), custom_call_target="tpu_custom_call" | custom-call | tf_op jit(solution)/shard_map/pick/pallas_call | solution.py:263
  1.9 29.8 %conditional.1 = (bf16[1,2,16,24,384]{4,3,2,1,0:T(8,128)(2,1)S(1)}) conditional(s32[]{:T(128)} %bitcast.6, (s32[4]{0:T(128)}, s32[1,4]{1,0:T(1,128)}, bf16[2,16,24,384]{3,2,1,0:T(8,128)(2,1)}, f32[384]{0:T(512)}, f32[384]{0:T(512)}, /*index=5*/bf16[3,3,1152,384]{3,2,1,0:T(8,128)(2,1)}) %tuple.48, (s32[4]{0:T(128)}, ...), branch_computations={%region_0.0_spmd, %region_1.0_spmd, %region_2.0_spmd, %region_3.0_... | conditional | bytes 8 | solution.py:303
  2.1 29.6 %conv_order_4.1 = bf16[2,16,24,384]{3,2,1,0:T(8,128)(2,1)S(1)} custom-call(s32[4]{0:T(128)} %get-tuple-element.109.slot_ref, s32[1,4]{1,0:T(1,128)} %get-tuple-element.110.margin_ref, bf16[2,16,24,384]{3,2,1,0:T(8,128)(2,1)} %get-tuple-element.111.x_ref, f32[384]{0:T(512)} %get-tuple-element.112.gain_ref, f32[384]{0:T(512)} %get-tuple-element.113.bias_ref, ...), custom_call_target="tpu_custom_call" | custom-call | tf_op jit(solution)/shard_map/cond/branch_4_fun/conv_order_4/pallas_call | solution.py:277
  31.6 0.8 %copy.20 = bf16[1,2,16,24,384]{4,3,2,1,0:T(8,128)(2,1)} copy(bf16[1,2,16,24,384]{4,3,2,1,0:T(8,128)(2,1)S(1)} %get-tuple-element.121) | data formatting | bytes 1179648

commit v3 on v2

--- a/solution.py
+++ b/solution.py
@@ -27,9 +27,9 @@
     return out
 
 
-def body(order, n_tile, slot_ref, margin_ref, x_ref, gain_ref, bias_ref, w_hbm, out_ref,
-         prev, rows_in, cols_in, corners_in, cols_out, w, act, z, acc,
-         send_small, recv_small, send_big, recv_big, w_sem):
+def body(order, n_tile, slot_ref, margin_ref, x_hbm, gain_ref, bias_ref, w_hbm, out_ref,
+         x_ref, prev, rows_in, cols_in, corners_in, cols_out, w, act, z, acc,
+         send_small, recv_small, send_big, recv_big, w_sem, x_sem):
     frames, core_h, core_w, channels = x_ref.shape
     n_group = len(order)
     grid_cols = n_tile // GRID_R
@@ -45,6 +45,8 @@
     nxt = table(group, following)
     before = table(group, preceding)
 
+    x_copy = pltpu.make_async_copy(x_hbm, x_ref, x_sem)
+    x_copy.start()
     for a in (2, 1, 0):
         pltpu.make_async_copy(w_hbm.at[a], w.at[a], w_sem.at[a]).start()
 
@@ -72,6 +74,7 @@
                 pl.semaphore_signal(barrier, inc=1, device_id={"group": peer, "tile": other},
                                     device_id_type=MESH)
 
+    x_copy.wait()
     for f in range(frames):
         edge = x_ref[f].astype(jnp.float32)
         cols_out[0, f] = edge[:, 0, :].astype(jnp.bfloat16)
@@ -125,18 +128,18 @@
     beta_left = kept(left)
     beta_right = kept(right)
 
-    def build(kind, f, source, slot):
-        def gated(v):
-            return jnp.where(not_first, v, 0.0) if kind else v
-
-        lanes = channels // 128
-
-        def store(at, v):
-            for c in range(lanes):
-                act[slot, c, at] = v[:, c * 128:(c + 1) * 128]
-
-        def fetch(at):
-            return jnp.concatenate([act[slot, c, at] for c in range(lanes)], axis=-1)
+    lanes = channels // 128
+
+    def gate(kind, v):
+        return jnp.where(not_first, v, 0.0) if kind else v
+
+    def put_act(slot, at, v):
+        for c in range(lanes):
+            act[slot, c, at] = v[:, c * 128:(c + 1) * 128]
+
+    def interior(kind, f, source, slot):
+        gated = functools.partial(gate, kind)
+        store = functools.partial(put_act, slot)
 
         store(pl.ds(0, pitch), jnp.zeros((pitch, channels), jnp.float32))
         store(pl.ds((core_h + 1) * pitch, pitch), jnp.zeros((pitch, channels), jnp.float32))
@@ -149,6 +152,14 @@
                 store(pl.ds(at, core_w), gated(activate(source[f, 4 * i + k], gain)))
             return carry
         lax.fori_loop(0, core_h // 4, one_row, 0)
+
+    def finish(kind, f, slot):
+        gated = functools.partial(gate, kind)
+        store = functools.partial(put_act, slot)
+
+        def fetch(at):
+            return jnp.concatenate([act[slot, c, at] for c in range(lanes)], axis=-1)
+
         for n, (step_r, step_c) in enumerate(DIRS):
             @pl.when(present(step_r, step_c))
             def _():
@@ -190,9 +201,11 @@
     def wait_w(a):
         pltpu.make_async_copy(w_hbm.at[a], w.at[a], w_sem.at[a]).wait()
 
+    interior(0, 0, x_ref, 0)
+    interior(0, 1, x_ref, 1)
     wait_rims(0)
-    build(0, 0, x_ref, 0)
-    build(0, 1, x_ref, 1)
+    finish(0, 0, 0)
+    finish(0, 1, 1)
     wait_w(2)
     wait_w(1)
     acc[...] = jnp.zeros(acc.shape, jnp.float32)
@@ -217,23 +230,28 @@
     wait_w(0)
     wait_rims(1)
     block_copy(1).wait_recv()
-    build(1, 1, prev, 1)
+    interior(1, 1, prev, 1)
+    finish(1, 1, 1)
     both(1, 1, 0)
-    block_copy(0).wait_recv()
-    build(1, 0, prev, 0)
-    single(0, 0, 0)
-
     bias = bias_ref[...].reshape(1, channels)
-    for s in range(frames):
-        for c in range(channels // 128):
+
+    def give(s):
+        for c in range(lanes):
             first = s * channels + c * 128
             act[s, c, pl.ds(0, core_h * core_w)] = acc[:, first:first + 128]
 
         def put(i, carry):
-            v = jnp.concatenate([act[s, c, pl.ds(i, core_w, stride=core_h)] for c in range(channels // 128)], axis=-1)
+            v = jnp.concatenate([act[s, c, pl.ds(i, core_w, stride=core_h)] for c in range(lanes)], axis=-1)
             out_ref[s, i] = (v + bias).astype(out_ref.dtype)
             return carry
-        lax.fori_loop(0, core_h, put, 0)
+        lax.fori_loop(0, core_h, put, 0, unroll=4)
+
+    give(1)
+    block_copy(0).wait_recv()
+    interior(1, 0, prev, 0)
+    finish(1, 0, 0)
+    single(0, 0, 0)
+    give(0)
 
     for kind in (0, 1):
         for n, (step_r, step_c) in enumerate(DIRS):
@@ -277,9 +295,10 @@
             return pl.pallas_call(
                 functools.partial(body, orders[k], n_tile),
                 out_shape=jax.ShapeDtypeStruct(x.shape, jnp.bfloat16),
-                in_specs=[smem, smem, vmem, vmem, vmem, pl.BlockSpec(memory_space=pl.ANY)],
+                in_specs=[smem, smem, pl.BlockSpec(memory_space=pl.ANY), vmem, vmem, pl.BlockSpec(memory_space=pl.ANY)],
                 out_specs=vmem,
                 scratch_shapes=[
+                    pltpu.VMEM((frames, core_h, core_w, channels), jnp.bfloat16),
                     pltpu.VMEM((frames, core_h, core_w, channels), jnp.bfloat16),
                     pltpu.VMEM((2, 2, frames, core_w, channels), jnp.bfloat16),
                     pltpu.VMEM((2, 2, frames, core_h, channels), jnp.bfloat16),
@@ -294,6 +313,7 @@
                     pltpu.SemaphoreType.DMA((2,)),
                     pltpu.SemaphoreType.DMA((2,)),
                     pltpu.SemaphoreType.DMA((3,)),
+                    pltpu.SemaphoreType.DMA,
                 ],
                 compiler_params=pltpu.CompilerParams(collective_id=k, has_side_effects=True),
                 name="conv_order_%d" % k,

time: 32.2 us -> 31 us (0.963)
  Pallas kernels: 30.8 us -> 29.4 us
    pallas_call x1, Pallas kernels: 29.6 us -> 28.2 us  [run(): pl.pallas_call(functools.partial(body, orders[k], n_tile), out_shape=jax....]
where the time goes in v3:
time: 31 us; the launch traced here: 31.1 us
  Pallas kernels  29.4 us (95%)
  local copies, waits for them, and re-layouts  0.82 us (3%)
  between operations  0.67 us (2%)
    pallas_call x1, Pallas kernels, run(): pl.pallas_call(functools.partial(body, orders[k], n_tile), out_shape=jax....  28.2 us
    pallas_call x1, Pallas kernels, local(): pl.pallas_call(functools.partial(pick, orders), out_shape=jax.ShapeDtypeS...  1.2 us
    unnamed x1, local copies, waits for them, and re-layouts  0.82 us

profile of v3, /device:TPU:0, one launch (start us, length us, event | category | flops | bytes accessed | tf_op | source)
XLA Modules:
  0.0 31.1 jit_solution(16918767379672447925)
XLA Ops:
  0.0 1.2 %pick.1 = s32[1]{0:T(128)} custom-call(s32[4]{0:T(128)} %slot_ref.1), custom_call_target="tpu_custom_call" | custom-call | tf_op jit(solution)/shard_map/pick/pallas_call | solution.py:281
  1.9 28.4 %conditional.1 = (bf16[1,2,16,24,384]{4,3,2,1,0:T(8,128)(2,1)S(1)}) conditional(s32[]{:T(128)} %bitcast.6, (s32[4]{0:T(128)}, s32[1,4]{1,0:T(1,128)}, bf16[2,16,24,384]{3,2,1,0:T(8,128)(2,1)}, f32[384]{0:T(512)}, f32[384]{0:T(512)}, /*index=5*/bf16[3,3,1152,384]{3,2,1,0:T(8,128)(2,1)}) %tuple.48, (s32[4]{0:T(128)}, ...), branch_computations={%region_0.0_spmd, %region_1.0_spmd, %region_2.0_spmd, %region_3.0_... | conditional | bytes 8 | solution.py:323
  1.9 28.2 %conv_order_2.1 = bf16[2,16,24,384]{3,2,1,0:T(8,128)(2,1)S(1)} custom-call(s32[4]{0:T(128)} %get-tuple-element.97.slot_ref, s32[1,4]{1,0:T(1,128)} %get-tuple-element.98.margin_ref, bf16[2,16,24,384]{3,2,1,0:T(8,128)(2,1)} %get-tuple-element.99.x_hbm, f32[384]{0:T(512)} %get-tuple-element.100.gain_ref, f32[384]{0:T(512)} %get-tuple-element.101.bias_ref, ...), custom_call_target="tpu_custom_call" | custom-call | tf_op jit(solution)/shard_map/cond/branch_2_fun/conv_order_2/pallas_call | solution.py:295
  30.3 0.8 %copy.20 = bf16[1,2,16,24,384]{4,3,2,1,0:T(8,128)(2,1)} copy(bf16[1,2,16,24,384]{4,3,2,1,0:T(8,128)(2,1)S(1)} %get-tuple-element.121) | data formatting | bytes 1179648
